TPU v7x, 128 devices: a whole 4x4x4 slice. The times are simulated.
128 devices in a mesh: row: 8 (over z, core), col: 16 (over x, y).
Axes of the slice: x: 4, y: 4, z: 4, core: 2. Of those that a mesh axis runs over, the one named last changes fastest.
Arguments:
- rate_terms: bfloat16 [6, 8192, 8192], P(None, 'row', 'col'), may hold values from -1 to 1
- populations: float32 [8192, 256], P(('row', 'col')), may hold values from 0.05 to 1
- temp_bins: int32 [256], replicated, may hold values from 0 to 63
- bin_coeffs: float32 [64, 6], replicated, may hold values from -1 to 1
Outputs:
- updated: float32 [8192, 256], P(('row', 'col'))
All inputs are finite; a program needn't handle non-finite values.
Results may differ from a plain program's by a relative error of at most 0.0011.
Values may be sent and summed in bfloat16 or wider, within the bound.
No kernel may reach another device: no remote copies, remote signals or barrier semaphores. Data moves between devices by JAX's collectives and lax.ppermute only.
A program may use at most 64 MiB of HBM per device.

v0:
```python
import math
import jax
import jax.numpy as jnp
from jax import lax
from jax.sharding import PartitionSpec as P

KRYLOV = 4
TAYLOR = 8
epsilon = 1e-06
step_size = 1.0


def body(rate_terms, populations, temp_bins, bin_coeffs):
    col_id = lax.axis_index("col")
    n_terms = rate_terms.shape[0]
    row_rows = rate_terms.shape[1]
    col_rows = rate_terms.shape[2]
    n_bins = bin_coeffs.shape[0]
    n_cells = populations.shape[1]
    onehot = (temp_bins[:, None] == jnp.arange(n_bins, dtype=jnp.int32)[None, :]).astype(
        jnp.float32
    )
    weights = jnp.dot(onehot, bin_coeffs, precision=lax.Precision.HIGHEST)
    weights_t = weights.T
    stacked = rate_terms.reshape(n_terms * row_rows, col_rows)

    def apply_rates(vector):
        rounded = vector.astype(jnp.bfloat16)
        gathered = lax.all_gather(rounded, ("row", "col"), axis=0, tiled=True)
        operand = lax.dynamic_slice_in_dim(gathered, col_id * col_rows, col_rows, 0)
        products = jnp.dot(stacked, operand, preferred_element_type=jnp.float32).reshape(
            n_terms, row_rows, n_cells
        )
        partial_value = jnp.sum(products * weights_t[:, None, :], axis=0)
        return lax.psum_scatter(partial_value, "col", scatter_dimension=0, tiled=True)

    def norm_of(vector):
        squares = lax.psum(jnp.sum(vector * vector, axis=0), ("row", "col"))
        return jnp.sqrt(squares + epsilon)

    force = apply_rates(populations)
    scale_norm = norm_of(force)
    basis = [force / scale_norm[None, :]]
    zero_row = jnp.zeros((n_cells,), jnp.float32)
    hessen = [[zero_row for j in range(KRYLOV)] for i in range(KRYLOV)]
    for j in range(KRYLOV):
        fresh = apply_rates(basis[j])
        for i in range(j + 1):
            correlation = lax.psum(jnp.sum(basis[i] * fresh, axis=0), ("row", "col"))
            fresh = fresh - correlation[None, :] * basis[i]
            hessen[i][j] = correlation
        if j < KRYLOV - 1:
            length = norm_of(fresh)
            hessen[j + 1][j] = length
            basis.append(fresh / length[None, :])
    hmat = jnp.stack([jnp.stack(line) for line in hessen]) * step_size
    first_unit = jnp.zeros((KRYLOV, n_cells), jnp.float32).at[0].set(1.0)
    coeffs = first_unit / float(math.factorial(TAYLOR + 1))
    for k in range(TAYLOR - 1, -1, -1):
        coeffs = jnp.sum(hmat * coeffs[None, :, :], axis=1) + first_unit / float(
            math.factorial(k + 1)
        )
    update = jnp.zeros(populations.shape, jnp.float32)
    for i in range(KRYLOV):
        update = update + coeffs[i][None, :] * basis[i]
    return populations + step_size * scale_norm[None, :] * update


def solution(mesh):
    placed = (P(None, "row", "col"), P(("row", "col"), None), P(), P())
    return jax.shard_map(
        body, mesh=mesh, in_specs=placed, out_specs=P(("row", "col"), None), check_vma=False
    )
```

profile of v0, /device:TPU:1, one launch (start us, length us, event | category | flops | bytes accessed | tf_op | source)
XLA Modules:
  0.0 1696.6 jit_solution(16298154041316169169)
XLA Ops:
  9.0 71.7 %all-gather.6.cloned.1.call-done = bf16[8192,256]{1,0:T(8,128)(2,1)} async-done(((bf16[64,256]{1,0:T(8,128)(2,1)}), bf16[8192,256]{1,0:T(8,128)(2,1)}) %all-gather.6.cloned.1.call-update) | async-done | bytes 4194320 | tf_op jit(solution)/shard_map/all_gather | solution.py:29
  80.6 7.4 convolution_bitcast_fusion.4
  88.0 6.5 copy.11
  99.0 69.5 %reduce-scatter.6.cloned.1.call-done = f32[64,256]{1,0:T(8,128)} async-done(((f32[1024,256]{1,0:T(8,128)}), f32[64,256]{1,0:T(8,128)}) %reduce-scatter.6.cloned.1.call-update) | async-done | bytes 65552 | tf_op jit(solution)/shard_map/reduce_scatter | solution.py:35
  169.4 66.1 %psum.98 = f32[256]{0:T(256)S(1)} all-reduce(f32[256]{0:T(256)S(1)} %multiply_reduce_fusion.18), channel_id=1, replica_groups=mesh['row'=8,'col'=16] {'row','col'}, use_global_device_ids=true, to_apply=%region_3.0 | all-reduce | flops 256 | bytes 2048 | tf_op jit(solution)/shard_map/psum | solution.py:38
  237.1 63.4 %all-gather.8.cloned.1.call-done = bf16[8192,256]{1,0:T(8,128)(2,1)} async-done(((bf16[64,256]{1,0:T(8,128)(2,1)}), bf16[8192,256]{1,0:T(8,128)(2,1)}) %all-gather.8.cloned.1.call-update) | async-done | bytes 4194320 | tf_op jit(solution)/shard_map/all_gather | solution.py:29
  300.5 7.4 convolution_bitcast_fusion.3
  307.9 6.5 copy.12
  318.9 69.5 %reduce-scatter.8.cloned.1.call-done = f32[64,256]{1,0:T(8,128)} async-done(((f32[1024,256]{1,0:T(8,128)}), f32[64,256]{1,0:T(8,128)}) %reduce-scatter.8.cloned.1.call-update) | async-done | bytes 65552 | tf_op jit(solution)/shard_map/reduce_scatter | solution.py:35
  389.3 66.1 %psum.99 = f32[256]{0:T(256)S(1)} all-reduce(f32[256]{0:T(256)S(1)} %multiply_reduce_fusion.17), channel_id=1, replica_groups=mesh['row'=8,'col'=16] {'row','col'}, use_global_device_ids=true, to_apply=%region_7.0 | all-reduce | flops 256 | bytes 2048 | tf_op jit(solution)/shard_map/psum | solution.py:49
  456.3 62.5 %psum.100 = f32[256]{0:T(256)S(1)} all-reduce(f32[256]{0:T(256)S(1)} %multiply_reduce_fusion.16), channel_id=1, replica_groups=mesh['row'=8,'col'=16] {'row','col'}, use_global_device_ids=true, to_apply=%region_9.0 | all-reduce | flops 256 | bytes 2048 | tf_op jit(solution)/shard_map/psum | solution.py:38
  520.5 63.9 %all-gather.10.cloned.1.call-done = bf16[8192,256]{1,0:T(8,128)(2,1)} async-done(((bf16[64,256]{1,0:T(8,128)(2,1)}), bf16[8192,256]{1,0:T(8,128)(2,1)}) %all-gather.10.cloned.1.call-update) | async-done | bytes 4194320 | tf_op jit(solution)/shard_map/all_gather | solution.py:29
  584.4 7.4 convolution_bitcast_fusion.2
  602.8 69.5 %reduce-scatter.10.cloned.1.call-done = f32[64,256]{1,0:T(8,128)} async-done(((f32[1024,256]{1,0:T(8,128)}), f32[64,256]{1,0:T(8,128)}) %reduce-scatter.10.cloned.1.call-update) | async-done | bytes 65552 | tf_op jit(solution)/shard_map/reduce_scatter | solution.py:35
  673.2 66.1 %psum.101 = f32[256]{0:T(256)S(1)} all-reduce(f32[256]{0:T(256)S(1)} %multiply_reduce_fusion.15), channel_id=1, replica_groups=mesh['row'=8,'col'=16] {'row','col'}, use_global_device_ids=true, to_apply=%region_13.0 | all-reduce | flops 256 | bytes 2048 | tf_op jit(solution)/shard_map/psum | solution.py:49
  740.2 62.5 %psum.102 = f32[256]{0:T(256)S(1)} all-reduce(f32[256]{0:T(256)S(1)} %multiply_reduce_fusion.14), channel_id=1, replica_groups=mesh['row'=8,'col'=16] {'row','col'}, use_global_device_ids=true, to_apply=%region_15.0 | all-reduce | flops 256 | bytes 2048 | tf_op jit(solution)/shard_map/psum | solution.py:49
  803.6 64.0 %psum.103 = f32[256]{0:T(256)S(1)} all-reduce(f32[256]{0:T(256)S(1)} %get-tuple-element.21), channel_id=1, replica_groups=mesh['row'=8,'col'=16] {'row','col'}, use_global_device_ids=true, to_apply=%region_17.0 | all-reduce | flops 256 | bytes 2048 | tf_op jit(solution)/shard_map/psum | solution.py:38
  868.3 63.5 %all-gather.12.cloned.1.call-done = bf16[8192,256]{1,0:T(8,128)(2,1)} async-done(((bf16[64,256]{1,0:T(8,128)(2,1)}), bf16[8192,256]{1,0:T(8,128)(2,1)}) %all-gather.12.cloned.1.call-update) | async-done | bytes 4194320 | tf_op jit(solution)/shard_map/all_gather | solution.py:29
  931.8 7.4 convolution_bitcast_fusion.1
  950.2 69.5 %reduce-scatter.12.cloned.1.call-done = f32[64,256]{1,0:T(8,128)} async-done(((f32[1024,256]{1,0:T(8,128)}), f32[64,256]{1,0:T(8,128)}) %reduce-scatter.12.cloned.1.call-update) | async-done | bytes 65552 | tf_op jit(solution)/shard_map/reduce_scatter | solution.py:35
  1020.6 66.1 %psum.104 = f32[256]{0:T(256)S(1)} all-reduce(f32[256]{0:T(256)S(1)} %multiply_reduce_fusion.12), channel_id=1, replica_groups=mesh['row'=8,'col'=16] {'row','col'}, use_global_device_ids=true, to_apply=%region_21.0 | all-reduce | flops 256 | bytes 2048 | tf_op jit(solution)/shard_map/psum | solution.py:49
  1087.6 62.5 %psum.105 = f32[256]{0:T(256)S(1)} all-reduce(f32[256]{0:T(256)S(1)} %multiply_reduce_fusion.11), channel_id=1, replica_groups=mesh['row'=8,'col'=16] {'row','col'}, use_global_device_ids=true, to_apply=%region_23.0 | all-reduce | flops 256 | bytes 2048 | tf_op jit(solution)/shard_map/psum | solution.py:49
  1151.0 64.3 %psum.106 = f32[256]{0:T(256)S(1)} all-reduce(f32[256]{0:T(256)S(1)} %get-tuple-element.19), channel_id=1, replica_groups=mesh['row'=8,'col'=16] {'row','col'}, use_global_device_ids=true, to_apply=%region_25.0 | all-reduce | flops 256 | bytes 2048 | tf_op jit(solution)/shard_map/psum | solution.py:49
  1215.2 62.5 %psum.107 = f32[256]{0:T(256)S(1)} all-reduce(f32[256]{0:T(256)S(1)} %multiply_reduce_fusion.9), channel_id=1, replica_groups=mesh['row'=8,'col'=16] {'row','col'}, use_global_device_ids=true, to_apply=%region_27.0 | all-reduce | flops 256 | bytes 2048 | tf_op jit(solution)/shard_map/psum | solution.py:38
  1278.5 64.1 %all-gather.14.cloned.1.call-done = bf16[8192,256]{1,0:T(8,128)(2,1)} async-done(((bf16[64,256]{1,0:T(8,128)(2,1)}), bf16[8192,256]{1,0:T(8,128)(2,1)}) %all-gather.14.cloned.1.call-update) | async-done | bytes 4194320 | tf_op jit(solution)/shard_map/all_gather | solution.py:29
  1342.6 7.4 convolution_bitcast_fusion
  1350.0 6.5 copy.15
  1361.1 69.5 %reduce-scatter.14.cloned.1.call-done = f32[64,256]{1,0:T(8,128)} async-done(((f32[1024,256]{1,0:T(8,128)}), f32[64,256]{1,0:T(8,128)}) %reduce-scatter.14.cloned.1.call-update) | async-done | bytes 65552 | tf_op jit(solution)/shard_map/reduce_scatter | solution.py:35
  1431.5 66.1 %psum.108 = f32[256]{0:T(256)S(1)} all-reduce(f32[256]{0:T(256)S(1)} %multiply_reduce_fusion.8), channel_id=1, replica_groups=mesh['row'=8,'col'=16] {'row','col'}, use_global_device_ids=true, to_apply=%region_31.0 | all-reduce | flops 256 | bytes 2048 | tf_op jit(solution)/shard_map/psum | solution.py:49
  1498.5 62.5 %psum.109 = f32[256]{0:T(256)S(1)} all-reduce(f32[256]{0:T(256)S(1)} %multiply_reduce_fusion.7), channel_id=1, replica_groups=mesh['row'=8,'col'=16] {'row','col'}, use_global_device_ids=true, to_apply=%region_33.0 | all-reduce | flops 256 | bytes 2048 | tf_op jit(solution)/shard_map/psum | solution.py:49
  1561.9 64.0 %psum.110 = f32[256]{0:T(256)S(1)} all-reduce(f32[256]{0:T(256)S(1)} %get-tuple-element.17), channel_id=1, replica_groups=mesh['row'=8,'col'=16] {'row','col'}, use_global_device_ids=true, to_apply=%region_35.0 | all-reduce | flops 256 | bytes 2048 | tf_op jit(solution)/shard_map/psum | solution.py:49
  1626.0 62.5 %psum.111 = f32[1,256]{1,0:T(1,128)S(1)} all-reduce(f32[1,256]{1,0:T(1,128)S(1)} %bitcast.72), channel_id=1, replica_groups=mesh['row'=8,'col'=16] {'row','col'}, use_global_device_ids=true, to_apply=%region_37.0 | all-reduce | flops 256 | bytes 2048 | tf_op jit(solution)/shard_map/psum | solution.py:49
  (101 shorter events, 54.0 us)
Async XLA Ops:
  6.5 1.6 copy-start
  6.5 74.1 %all-gather.6.cloned.1.call-start = ((), (), s32[]{:S(2)}) async-start(), calls=%async_computation.5 | async-start | bytes 4227072 | tf_op jit(solution)/shard_map/all_gather | solution.py:29
  8.0 160.5 %reduce-scatter.6.cloned.1.call-start = ((), (), s32[]{:S(2)}) async-start(), calls=%async_computation.6 | async-start | bytes 1114112 | tf_op jit(solution)/shard_map/reduce_scatter | solution.py:35
  98.9 201.5 %all-gather.8.cloned.1.call-start = ((), (), s32[]{:S(2)}) async-start(), calls=%async_computation.7 | async-start | bytes 4227072 | tf_op jit(solution)/shard_map/all_gather | solution.py:29
  237.0 151.4 %reduce-scatter.8.cloned.1.call-start = ((), (), s32[]{:S(2)}) async-start(), calls=%async_computation.8 | async-start | bytes 1114112 | tf_op jit(solution)/shard_map/reduce_scatter | solution.py:35
  314.4 74.0 %copy-start.2 = (f32[64,256]{1,0:T(8,128)S(1)}, f32[64,256]{1,0:T(8,128)}, u32[]{:S(2)}) copy-start(f32[64,256]{1,0:T(8,128)} %reduce-scatter.6.cloned.1.call-done) | copy-start | bytes 196612
  318.8 265.6 %all-gather.10.cloned.1.call-start = ((), (), s32[]{:S(2)}) async-start(), calls=%async_computation.9 | async-start | bytes 4227072 | tf_op jit(solution)/shard_map/all_gather | solution.py:29
  520.3 152.1 %reduce-scatter.10.cloned.1.call-start = ((), (), s32[]{:S(2)}) async-start(), calls=%async_computation.10 | async-start | bytes 1114112 | tf_op jit(solution)/shard_map/reduce_scatter | solution.py:35
  598.4 141.0 %copy-start.3 = (f32[64,256]{1,0:T(8,128)S(1)}, f32[64,256]{1,0:T(8,128)}, u32[]{:S(2)}) copy-start(f32[64,256]{1,0:T(8,128)} %reduce-scatter.8.cloned.1.call-done) | copy-start | bytes 196612
  602.7 329.1 %all-gather.12.cloned.1.call-start = ((), (), s32[]{:S(2)}) async-start(), calls=%async_computation.11 | async-start | bytes 4227072 | tf_op jit(solution)/shard_map/all_gather | solution.py:29
  868.3 151.4 %reduce-scatter.12.cloned.1.call-start = ((), (), s32[]{:S(2)}) async-start(), calls=%async_computation.12 | async-start | bytes 1114112 | tf_op jit(solution)/shard_map/reduce_scatter | solution.py:35
  950.1 392.5 %all-gather.14.cloned.1.call-start = ((), (), s32[]{:S(2)}) async-start(), calls=%async_computation.13 | async-start | bytes 4227072 | tf_op jit(solution)/shard_map/all_gather | solution.py:29
  1278.5 152.2 %reduce-scatter.14.cloned.1.call-start = ((), (), s32[]{:S(2)}) async-start(), calls=%async_computation.14 | async-start | bytes 1114112 | tf_op jit(solution)/shard_map/reduce_scatter | solution.py:35
  1350.0 339.7 %copy-start.1 = (f32[64,6]{0,1:T(8,128)S(1)}, f32[64,6]{0,1:T(8,128)}, u32[]{:S(2)}) copy-start(f32[64,6]{0,1:T(8,128)} %param.9) | copy-start | bytes 4612
  1356.6 332.1 %copy-start.12 = (f32[4,256]{1,0:T(4,128)S(1)}, f32[4,256]{1,0:T(4,128)}, u32[]{:S(2)}) copy-start(f32[4,256]{1,0:T(4,128)} %constant.71.clone.1) | copy-start | bytes 12292
  1356.6 332.1 %copy-start.11 = (f32[4,256]{1,0:T(4,128)S(1)}, f32[4,256]{1,0:T(4,128)}, u32[]{:S(2)}) copy-start(f32[4,256]{1,0:T(4,128)} %constant.72.clone.1) | copy-start | bytes 12292
  1356.6 332.2 %copy-start.10 = (f32[4,256]{1,0:T(4,128)S(1)}, f32[4,256]{1,0:T(4,128)}, u32[]{:S(2)}) copy-start(f32[4,256]{1,0:T(4,128)} %constant.73.clone.1) | copy-start | bytes 12292
  1356.6 332.2 %copy-start.9 = (f32[4,256]{1,0:T(4,128)S(1)}, f32[4,256]{1,0:T(4,128)}, u32[]{:S(2)}) copy-start(f32[4,256]{1,0:T(4,128)} %constant.74.clone.1) | copy-start | bytes 12292
  1356.6 332.3 %copy-start.8 = (f32[4,256]{1,0:T(4,128)S(1)}, f32[4,256]{1,0:T(4,128)}, u32[]{:S(2)}) copy-start(f32[4,256]{1,0:T(4,128)} %constant.75.clone.1) | copy-start | bytes 12292
  1356.6 332.3 %copy-start.7 = (f32[4,256]{1,0:T(4,128)S(1)}, f32[4,256]{1,0:T(4,128)}, u32[]{:S(2)}) copy-start(f32[4,256]{1,0:T(4,128)} %constant.76.clone.1) | copy-start | bytes 12292
  1356.6 332.3 %copy-start.6 = (f32[4,256]{1,0:T(4,128)S(1)}, f32[4,256]{1,0:T(4,128)}, u32[]{:S(2)}) copy-start(f32[4,256]{1,0:T(4,128)} %constant.77.clone.1) | copy-start | bytes 12292
  1356.6 332.4 %copy-start.5 = (f32[4,256]{1,0:T(4,128)S(1)}, f32[4,256]{1,0:T(4,128)}, u32[]{:S(2)}) copy-start(f32[4,256]{1,0:T(4,128)} %constant.78.clone.1) | copy-start | bytes 12292
  1356.6 332.4 %copy-start.4 = (f32[64,256]{1,0:T(8,128)S(1)}, f32[64,256]{1,0:T(8,128)}, u32[]{:S(2)}) copy-start(f32[64,256]{1,0:T(8,128)} %param.7) | copy-start | bytes 196612
Sparse Core Ops, SparseCore 0:
  10.5 70.1 all-gather.5
  99.1 69.4 reduce-scatter.5
  237.1 63.3 all-gather.7
  318.9 69.4 reduce-scatter.7
  520.4 64.0 all-gather.9
  602.9 69.4 reduce-scatter.9
  868.4 63.3 all-gather.11
  950.3 69.4 reduce-scatter.11
  1278.6 64.0 all-gather.13
  1361.2 69.3 reduce-scatter.13
where the time goes:
time: 1700 us
  blocking collectives  898 us (53%)
  waiting for transfers between devices  674 us (40%)
  other arithmetic  39.3 us (2%)
  matrix products  37.9 us (2%)
  local copies, waits for them, and re-layouts  32.7 us (2%)
    psum x10, blocking collectives, body(): correlation = lax.psum(jnp.sum(basis[i] * fresh, axis=0), ('row', 'col'))  643 us
    reduce_scatter x5, waiting for transfers between devices, apply_rates(): lax.psum_scatter(partial_value, 'col', scatter_dimension=0, tiled=True)  348 us
    all_gather x5, waiting for transfers between devices, apply_rates(): gathered = lax.all_gather(rounded, ('row', 'col'), axis=0, tiled=True)  327 us
    psum x4, blocking collectives, norm_of(): squares = lax.psum(jnp.sum(vector * vector, axis=0), ('row', 'col'))  255 us
    dot_general x5, matrix products, apply_rates(): jnp.dot(stacked, operand, preferred_element_type=jnp.float32)  37 us
  transfers between devices with their start and end apart: 10, of which 10 were waited for; matrix products, arithmetic and copies ran while one was open for 0% of the time, Pallas kernels for 0%

commit v1 on v0

--- a/solution.py
+++ b/solution.py
@@ -46,7 +46,7 @@
     for j in range(KRYLOV):
         fresh = apply_rates(basis[j])
         for i in range(j + 1):
-            correlation = lax.psum(jnp.sum(basis[i] * fresh, axis=0), ("row", "col"))
+            correlation = lax.psum(lax.psum(jnp.sum(basis[i] * fresh, axis=0), "col"), "row")
             fresh = fresh - correlation[None, :] * basis[i]
             hessen[i][j] = correlation
         if j < KRYLOV - 1:

time: 1700 us -> 1550 us (0.912)
  blocking collectives: 898 us -> 754 us
    psum x10 -> x20, blocking collectives: 643 us -> 500 us  [the longest x10 299 us: body(): lax.psum(jnp.sum(basis[i] * fresh, axis=0), 'col')]
where the time goes in v1:
time: 1550 us
  blocking collectives  754 us (49%)
  waiting for transfers between devices  675 us (44%)
  other arithmetic  39.3 us (3%)
  matrix products  37.9 us (2%)
  local copies, waits for them, and re-layouts  32.7 us (2%)
    reduce_scatter x5, waiting for transfers between devices, apply_rates(): lax.psum_scatter(partial_value, 'col', scatter_dimension=0, tiled=True)  348 us
    all_gather x5, waiting for transfers between devices, apply_rates(): gathered = lax.all_gather(rounded, ('row', 'col'), axis=0, tiled=True)  327 us
    psum x10, blocking collectives, body(): lax.psum(jnp.sum(basis[i] * fresh, axis=0), 'col')  299 us
    psum x4, blocking collectives, norm_of(): squares = lax.psum(jnp.sum(vector * vector, axis=0), ('row', 'col'))  253 us
    psum x10, blocking collectives, body(): lax.psum(lax.psum(jnp.sum(basis[i] * fresh, axis=0), 'col'), 'row')  201 us
    dot_general x5, matrix products, apply_rates(): jnp.dot(stacked, operand, preferred_element_type=jnp.float32)  37 us
    dot_general x5, local copies, waits for them, and re-layouts, apply_rates(): jnp.dot(stacked, operand, preferred_element_type=jnp.float32)  32.6 us
  transfers between devices with their start and end apart: 10, of which 10 were waited for; matrix products, arithmetic and copies ran while one was open for 0% of the time, Pallas kernels for 0%

profile of v1, /device:TPU:1, one launch (start us, length us, event | category | flops | bytes accessed | tf_op | source)
XLA Modules:
  0.0 1552.7 jit_solution(1463091828336133136)
XLA Ops:
  9.0 71.7 %all-gather.6.cloned.1.call-done = bf16[8192,256]{1,0:T(8,128)(2,1)} async-done(((bf16[64,256]{1,0:T(8,128)(2,1)}), bf16[8192,256]{1,0:T(8,128)(2,1)}) %all-gather.6.cloned.1.call-update) | async-done | bytes 4194320 | tf_op jit(solution)/shard_map/all_gather | solution.py:29
  99.0 69.5 %reduce-scatter.6.cloned.1.call-done = f32[64,256]{1,0:T(8,128)} async-done(((f32[1024,256]{1,0:T(8,128)}), f32[64,256]{1,0:T(8,128)}) %reduce-scatter.6.cloned.1.call-update) | async-done | bytes 65552 | tf_op jit(solution)/shard_map/reduce_scatter | solution.py:35
  169.4 66.1 %psum.168 = f32[256]{0:T(256)S(1)} all-reduce(f32[256]{0:T(256)S(1)} %multiply_reduce_fusion.18), channel_id=1, replica_groups=mesh['row'=8,'col'=16] {'row','col'}, use_global_device_ids=true, to_apply=%region_3.0 | all-reduce | flops 256 | bytes 2048 | tf_op jit(solution)/shard_map/psum | solution.py:38
  237.1 63.4 %all-gather.8.cloned.1.call-done = bf16[8192,256]{1,0:T(8,128)(2,1)} async-done(((bf16[64,256]{1,0:T(8,128)(2,1)}), bf16[8192,256]{1,0:T(8,128)(2,1)}) %all-gather.8.cloned.1.call-update) | async-done | bytes 4194320 | tf_op jit(solution)/shard_map/all_gather | solution.py:29
  318.9 69.5 %reduce-scatter.8.cloned.1.call-done = f32[64,256]{1,0:T(8,128)} async-done(((f32[1024,256]{1,0:T(8,128)}), f32[64,256]{1,0:T(8,128)}) %reduce-scatter.8.cloned.1.call-update) | async-done | bytes 65552 | tf_op jit(solution)/shard_map/reduce_scatter | solution.py:35
  389.3 30.9 %psum.169 = f32[256]{0:T(256)S(1)} all-reduce(f32[256]{0:T(256)S(1)} %multiply_reduce_fusion.17), channel_id=1, replica_groups=mesh['row'=8,'col'=16] {'col'}, use_global_device_ids=true, to_apply=%region_7.0 | all-reduce | flops 256 | bytes 2048 | tf_op jit(solution)/shard_map/psum | solution.py:49
  420.2 21.4 %psum.170 = f32[256]{0:T(256)S(1)} all-reduce(f32[256]{0:T(256)S(1)} %psum.169), channel_id=1, replica_groups=mesh['row'=8,'col'=16] {'row'}, use_global_device_ids=true, to_apply=%region_8.0 | all-reduce | flops 256 | bytes 2048 | tf_op jit(solution)/shard_map/psum | solution.py:49
  442.5 61.9 %psum.171 = f32[256]{0:T(256)S(1)} all-reduce(f32[256]{0:T(256)S(1)} %multiply_reduce_fusion.16), channel_id=1, replica_groups=mesh['row'=8,'col'=16] {'row','col'}, use_global_device_ids=true, to_apply=%region_10.0 | all-reduce | flops 256 | bytes 2048 | tf_op jit(solution)/shard_map/psum | solution.py:38
  506.0 64.0 %all-gather.10.cloned.1.call-done = bf16[8192,256]{1,0:T(8,128)(2,1)} async-done(((bf16[64,256]{1,0:T(8,128)(2,1)}), bf16[8192,256]{1,0:T(8,128)(2,1)}) %all-gather.10.cloned.1.call-update) | async-done | bytes 4194320 | tf_op jit(solution)/shard_map/all_gather | solution.py:29
  588.4 69.5 %reduce-scatter.10.cloned.1.call-done = f32[64,256]{1,0:T(8,128)} async-done(((f32[1024,256]{1,0:T(8,128)}), f32[64,256]{1,0:T(8,128)}) %reduce-scatter.10.cloned.1.call-update) | async-done | bytes 65552 | tf_op jit(solution)/shard_map/reduce_scatter | solution.py:35
  658.7 31.1 %psum.172 = f32[256]{0:T(256)S(1)} all-reduce(f32[256]{0:T(256)S(1)} %multiply_reduce_fusion.15), channel_id=1, replica_groups=mesh['row'=8,'col'=16] {'col'}, use_global_device_ids=true, to_apply=%region_14.0 | all-reduce | flops 256 | bytes 2048 | tf_op jit(solution)/shard_map/psum | solution.py:49
  689.8 21.5 %psum.173 = f32[256]{0:T(256)S(1)} all-reduce(f32[256]{0:T(256)S(1)} %psum.172), channel_id=1, replica_groups=mesh['row'=8,'col'=16] {'row'}, use_global_device_ids=true, to_apply=%region_15.0 | all-reduce | flops 256 | bytes 2048 | tf_op jit(solution)/shard_map/psum | solution.py:49
  712.2 28.8 %psum.174 = f32[256]{0:T(256)S(1)} all-reduce(f32[256]{0:T(256)S(1)} %multiply_reduce_fusion.14), channel_id=1, replica_groups=mesh['row'=8,'col'=16] {'col'}, use_global_device_ids=true, to_apply=%region_17.0 | all-reduce | flops 256 | bytes 2048 | tf_op jit(solution)/shard_map/psum | solution.py:49
  741.0 18.9 %psum.175 = f32[256]{0:T(256)S(1)} all-reduce(f32[256]{0:T(256)S(1)} %psum.174), channel_id=1, replica_groups=mesh['row'=8,'col'=16] {'row'}, use_global_device_ids=true, to_apply=%region_18.0 | all-reduce | flops 256 | bytes 2048 | tf_op jit(solution)/shard_map/psum | solution.py:49
  760.8 63.2 %psum.176 = f32[256]{0:T(256)S(1)} all-reduce(f32[256]{0:T(256)S(1)} %get-tuple-element.21), channel_id=1, replica_groups=mesh['row'=8,'col'=16] {'row','col'}, use_global_device_ids=true, to_apply=%region_20.0 | all-reduce | flops 256 | bytes 2048 | tf_op jit(solution)/shard_map/psum | solution.py:38
  824.7 64.0 %all-gather.12.cloned.1.call-done = bf16[8192,256]{1,0:T(8,128)(2,1)} async-done(((bf16[64,256]{1,0:T(8,128)(2,1)}), bf16[8192,256]{1,0:T(8,128)(2,1)}) %all-gather.12.cloned.1.call-update) | async-done | bytes 4194320 | tf_op jit(solution)/shard_map/all_gather | solution.py:29
  907.1 69.5 %reduce-scatter.12.cloned.1.call-done = f32[64,256]{1,0:T(8,128)} async-done(((f32[1024,256]{1,0:T(8,128)}), f32[64,256]{1,0:T(8,128)}) %reduce-scatter.12.cloned.1.call-update) | async-done | bytes 65552 | tf_op jit(solution)/shard_map/reduce_scatter | solution.py:35
  977.5 30.9 %psum.177 = f32[256]{0:T(256)S(1)} all-reduce(f32[256]{0:T(256)S(1)} %multiply_reduce_fusion.12), channel_id=1, replica_groups=mesh['row'=8,'col'=16] {'col'}, use_global_device_ids=true, to_apply=%region_24.0 | all-reduce | flops 256 | bytes 2048 | tf_op jit(solution)/shard_map/psum | solution.py:49
  1008.4 21.4 %psum.178 = f32[256]{0:T(256)S(1)} all-reduce(f32[256]{0:T(256)S(1)} %psum.177), channel_id=1, replica_groups=mesh['row'=8,'col'=16] {'row'}, use_global_device_ids=true, to_apply=%region_25.0 | all-reduce | flops 256 | bytes 2048 | tf_op jit(solution)/shard_map/psum | solution.py:49
  1030.7 28.8 %psum.179 = f32[256]{0:T(256)S(1)} all-reduce(f32[256]{0:T(256)S(1)} %multiply_reduce_fusion.11), channel_id=1, replica_groups=mesh['row'=8,'col'=16] {'col'}, use_global_device_ids=true, to_apply=%region_27.0 | all-reduce | flops 256 | bytes 2048 | tf_op jit(solution)/shard_map/psum | solution.py:49
  1079.3 30.2 %psum.181 = f32[256]{0:T(256)S(1)} all-reduce(f32[256]{0:T(256)S(1)} %get-tuple-element.19), channel_id=1, replica_groups=mesh['row'=8,'col'=16] {'col'}, use_global_device_ids=true, to_apply=%region_30.0 | all-reduce | flops 256 | bytes 2048 | tf_op jit(solution)/shard_map/psum | solution.py:49
  1109.6 19.6 %psum.182 = f32[256]{0:T(256)S(1)} all-reduce(f32[256]{0:T(256)S(1)} %psum.181), channel_id=1, replica_groups=mesh['row'=8,'col'=16] {'row'}, use_global_device_ids=true, to_apply=%region_31.0 | all-reduce | flops 256 | bytes 2048 | tf_op jit(solution)/shard_map/psum | solution.py:49
  1129.3 62.0 %psum.183 = f32[256]{0:T(256)S(1)} all-reduce(f32[256]{0:T(256)S(1)} %multiply_reduce_fusion.9), channel_id=1, replica_groups=mesh['row'=8,'col'=16] {'row','col'}, use_global_device_ids=true, to_apply=%region_33.0 | all-reduce | flops 256 | bytes 2048 | tf_op jit(solution)/shard_map/psum | solution.py:38
  1192.0 64.1 %all-gather.14.cloned.1.call-done = bf16[8192,256]{1,0:T(8,128)(2,1)} async-done(((bf16[64,256]{1,0:T(8,128)(2,1)}), bf16[8192,256]{1,0:T(8,128)(2,1)}) %all-gather.14.cloned.1.call-update) | async-done | bytes 4194320 | tf_op jit(solution)/shard_map/all_gather | solution.py:29
  1274.5 69.6 %reduce-scatter.14.cloned.1.call-done = f32[64,256]{1,0:T(8,128)} async-done(((f32[1024,256]{1,0:T(8,128)}), f32[64,256]{1,0:T(8,128)}) %reduce-scatter.14.cloned.1.call-update) | async-done | bytes 65552 | tf_op jit(solution)/shard_map/reduce_scatter | solution.py:35
  1344.9 30.9 %psum.184 = f32[256]{0:T(256)S(1)} all-reduce(f32[256]{0:T(256)S(1)} %multiply_reduce_fusion.8), channel_id=1, replica_groups=mesh['row'=8,'col'=16] {'col'}, use_global_device_ids=true, to_apply=%region_37.0 | all-reduce | flops 256 | bytes 2048 | tf_op jit(solution)/shard_map/psum | solution.py:49
  1375.8 21.4 %psum.185 = f32[256]{0:T(256)S(1)} all-reduce(f32[256]{0:T(256)S(1)} %psum.184), channel_id=1, replica_groups=mesh['row'=8,'col'=16] {'row'}, use_global_device_ids=true, to_apply=%region_38.0 | all-reduce | flops 256 | bytes 2048 | tf_op jit(solution)/shard_map/psum | solution.py:49
  1398.1 28.8 %psum.186 = f32[256]{0:T(256)S(1)} all-reduce(f32[256]{0:T(256)S(1)} %multiply_reduce_fusion.7), channel_id=1, replica_groups=mesh['row'=8,'col'=16] {'col'}, use_global_device_ids=true, to_apply=%region_40.0 | all-reduce | flops 256 | bytes 2048 | tf_op jit(solution)/shard_map/psum | solution.py:49
  1446.8 30.2 %psum.188 = f32[256]{0:T(256)S(1)} all-reduce(f32[256]{0:T(256)S(1)} %get-tuple-element.17), channel_id=1, replica_groups=mesh['row'=8,'col'=16] {'col'}, use_global_device_ids=true, to_apply=%region_43.0 | all-reduce | flops 256 | bytes 2048 | tf_op jit(solution)/shard_map/psum | solution.py:49
  1477.0 19.6 %psum.189 = f32[256]{0:T(256)S(1)} all-reduce(f32[256]{0:T(256)S(1)} %psum.188), channel_id=1, replica_groups=mesh['row'=8,'col'=16] {'row'}, use_global_device_ids=true, to_apply=%region_44.0 | all-reduce | flops 256 | bytes 2048 | tf_op jit(solution)/shard_map/psum | solution.py:49
  1496.7 28.5 %psum.190 = f32[256]{0:T(256)S(1)} all-reduce(f32[256]{0:T(256)S(1)} %multiply_reduce_fusion.5), channel_id=1, replica_groups=mesh['row'=8,'col'=16] {'col'}, use_global_device_ids=true, to_apply=%region_46.0 | all-reduce | flops 256 | bytes 2048 | tf_op jit(solution)/shard_map/psum | solution.py:49
  1525.2 19.4 %psum.191 = f32[1,256]{1,0:T(1,128)S(1)} all-reduce(f32[1,256]{1,0:T(1,128)S(1)} %bitcast.76), channel_id=1, replica_groups=mesh['row'=8,'col'=16] {'row'}, use_global_device_ids=true, to_apply=%region_47.0 | all-reduce | flops 256 | bytes 2048 | tf_op jit(solution)/shard_map/psum | solution.py:49
  (111 shorter events, 148.3 us)
Async XLA Ops:
  6.5 1.6 copy-start
  6.5 74.1 %all-gather.6.cloned.1.call-start = ((), (), s32[]{:S(2)}) async-start(), calls=%async_computation.5 | async-start | bytes 4227072 | tf_op jit(solution)/shard_map/all_gather | solution.py:29
  8.0 160.5 %reduce-scatter.6.cloned.1.call-start = ((), (), s32[]{:S(2)}) async-start(), calls=%async_computation.6 | async-start | bytes 1114112 | tf_op jit(solution)/shard_map/reduce_scatter | solution.py:35
  98.9 201.5 %all-gather.8.cloned.1.call-start = ((), (), s32[]{:S(2)}) async-start(), calls=%async_computation.7 | async-start | bytes 4227072 | tf_op jit(solution)/shard_map/all_gather | solution.py:29
  237.0 151.4 %reduce-scatter.8.cloned.1.call-start = ((), (), s32[]{:S(2)}) async-start(), calls=%async_computation.8 | async-start | bytes 1114112 | tf_op jit(solution)/shard_map/reduce_scatter | solution.py:35
  314.4 74.0 %copy-start.2 = (f32[64,256]{1,0:T(8,128)S(1)}, f32[64,256]{1,0:T(8,128)}, u32[]{:S(2)}) copy-start(f32[64,256]{1,0:T(8,128)} %reduce-scatter.6.cloned.1.call-done) | copy-start | bytes 196612
  318.8 251.2 %all-gather.10.cloned.1.call-start = ((), (), s32[]{:S(2)}) async-start(), calls=%async_computation.9 | async-start | bytes 4227072 | tf_op jit(solution)/shard_map/all_gather | solution.py:29
  505.9 151.9 %reduce-scatter.10.cloned.1.call-start = ((), (), s32[]{:S(2)}) async-start(), calls=%async_computation.10 | async-start | bytes 1114112 | tf_op jit(solution)/shard_map/reduce_scatter | solution.py:35
  583.9 127.4 %copy-start.3 = (f32[64,256]{1,0:T(8,128)S(1)}, f32[64,256]{1,0:T(8,128)}, u32[]{:S(2)}) copy-start(f32[64,256]{1,0:T(8,128)} %reduce-scatter.8.cloned.1.call-done) | copy-start | bytes 196612
  588.3 300.4 %all-gather.12.cloned.1.call-start = ((), (), s32[]{:S(2)}) async-start(), calls=%async_computation.11 | async-start | bytes 4227072 | tf_op jit(solution)/shard_map/all_gather | solution.py:29
  824.7 151.9 %reduce-scatter.12.cloned.1.call-start = ((), (), s32[]{:S(2)}) async-start(), calls=%async_computation.12 | async-start | bytes 1114112 | tf_op jit(solution)/shard_map/reduce_scatter | solution.py:35
  907.0 349.0 %all-gather.14.cloned.1.call-start = ((), (), s32[]{:S(2)}) async-start(), calls=%async_computation.13 | async-start | bytes 4227072 | tf_op jit(solution)/shard_map/all_gather | solution.py:29
  1191.9 152.1 %reduce-scatter.14.cloned.1.call-start = ((), (), s32[]{:S(2)}) async-start(), calls=%async_computation.14 | async-start | bytes 1114112 | tf_op jit(solution)/shard_map/reduce_scatter | solution.py:35
  1263.4 282.4 %copy-start.1 = (f32[64,6]{0,1:T(8,128)S(1)}, f32[64,6]{0,1:T(8,128)}, u32[]{:S(2)}) copy-start(f32[64,6]{0,1:T(8,128)} %param.9) | copy-start | bytes 4612
  1270.0 274.8 %copy-start.12 = (f32[4,256]{1,0:T(4,128)S(1)}, f32[4,256]{1,0:T(4,128)}, u32[]{:S(2)}) copy-start(f32[4,256]{1,0:T(4,128)} %constant.71.clone.1) | copy-start | bytes 12292
  1270.0 274.8 %copy-start.11 = (f32[4,256]{1,0:T(4,128)S(1)}, f32[4,256]{1,0:T(4,128)}, u32[]{:S(2)}) copy-start(f32[4,256]{1,0:T(4,128)} %constant.72.clone.1) | copy-start | bytes 12292
  1270.0 274.8 %copy-start.10 = (f32[4,256]{1,0:T(4,128)S(1)}, f32[4,256]{1,0:T(4,128)}, u32[]{:S(2)}) copy-start(f32[4,256]{1,0:T(4,128)} %constant.73.clone.1) | copy-start | bytes 12292
  1270.0 274.9 %copy-start.9 = (f32[4,256]{1,0:T(4,128)S(1)}, f32[4,256]{1,0:T(4,128)}, u32[]{:S(2)}) copy-start(f32[4,256]{1,0:T(4,128)} %constant.74.clone.1) | copy-start | bytes 12292
  1270.0 274.9 %copy-start.8 = (f32[4,256]{1,0:T(4,128)S(1)}, f32[4,256]{1,0:T(4,128)}, u32[]{:S(2)}) copy-start(f32[4,256]{1,0:T(4,128)} %constant.75.clone.1) | copy-start | bytes 12292
  1270.0 275.0 %copy-start.7 = (f32[4,256]{1,0:T(4,128)S(1)}, f32[4,256]{1,0:T(4,128)}, u32[]{:S(2)}) copy-start(f32[4,256]{1,0:T(4,128)} %constant.76.clone.1) | copy-start | bytes 12292
  1270.0 275.0 %copy-start.6 = (f32[4,256]{1,0:T(4,128)S(1)}, f32[4,256]{1,0:T(4,128)}, u32[]{:S(2)}) copy-start(f32[4,256]{1,0:T(4,128)} %constant.77.clone.1) | copy-start | bytes 12292
  1270.0 275.0 %copy-start.5 = (f32[4,256]{1,0:T(4,128)S(1)}, f32[4,256]{1,0:T(4,128)}, u32[]{:S(2)}) copy-start(f32[4,256]{1,0:T(4,128)} %constant.78.clone.1) | copy-start | bytes 12292
  1270.0 275.1 %copy-start.4 = (f32[64,256]{1,0:T(8,128)S(1)}, f32[64,256]{1,0:T(8,128)}, u32[]{:S(2)}) copy-start(f32[64,256]{1,0:T(8,128)} %param.7) | copy-start | bytes 196612
Sparse Core Ops, SparseCore 0:
  10.5 70.1 all-gather.5
  99.1 69.4 reduce-scatter.5
  237.1 63.3 all-gather.7
  318.9 69.4 reduce-scatter.7
  506.0 63.9 all-gather.9
  588.4 69.3 reduce-scatter.9
  824.8 63.8 all-gather.11
  907.2 69.4 reduce-scatter.11
  1192.0 63.9 all-gather.13
  1274.6 69.4 reduce-scatter.13
